TPU v7x, 128 devices: a whole 4x4x4 slice. The times are simulated.
128 devices in a mesh: side: 2 (over z_lo), group: 2 (over z_hi), shard: 32 (over x, y, core).
Axes of the slice: x: 4, y: 4, z: 4 (z_hi: 2, z_lo: 2; z = z_hi * 2 + z_lo), core: 2. Of those that a mesh axis runs over, the one named last changes fastest.
Arguments:
- grad_parts: bfloat16 [4, 4, 7168, 2048], P(('side', 'group'), None, 'shard'), may hold values from -6 to 6
- master: float32 [4, 7168, 2048], P(('side', 'group'), 'shard'), may hold values from -6 to 6
- moment: float32 [4, 7168, 2048], P(('side', 'group'), 'shard'), may hold values from -4 to 4
- variance: float32 [4, 7168, 2048], P(('side', 'group'), 'shard'), may hold values from 0.0004 to 0.04
- plan: int32 [4], replicated, may hold values from 0 to 3, each once
- step: int32 [4], replicated, may hold values from 1 to 16
Outputs:
- new_master: float32 [4, 7168, 2048], P(('side', 'group'), 'shard')
- new_moment: float32 [4, 7168, 2048], P(('side', 'group'), 'shard')
- new_variance: float32 [4, 7168, 2048], P(('side', 'group'), 'shard')
- rollout_weights: bfloat16 [4, 2048, 7168], P(None, 'shard')
Inputs may be any that keep to these rules, and one draw needn't show every extreme that they name: `plan`: a permutation of the slots; slot s belongs to owner group s (groups numbered side-major).
All inputs are finite; a program needn't handle non-finite values.
Results may differ from a plain program's by a relative error of at most 0.0075.
Values may be sent and summed in bfloat16 or wider, within the bound.
A program may use at most 128 MiB of HBM per device.

v0:
```python
import jax
import jax.numpy as jnp
from jax import lax
from jax.sharding import PartitionSpec as P

BETA_ONE = 0.9
BETA_TWO = 0.999
LEARN = 0.1
DECAY = 0.1
EPSILON = 1e-08


def from_root(shard, axis, root):
    mine = lax.axis_index(axis) == root
    return lax.psum(jnp.where(mine, shard, jnp.zeros_like(shard)), axis)


def spread(local, plan, total):
    owned = local.shape[0]
    start = jnp.zeros((total,) + local.shape[1:], local.dtype)

    def one_matrix(index, result):
        slot = plan[index]
        root = slot // owned
        piece = lax.dynamic_index_in_dim(local, slot % owned, 0, keepdims=False)
        got = from_root(piece, ("side", "group"), root)
        return lax.dynamic_update_index_in_dim(result, got, index, 0)

    return lax.fori_loop(0, total, one_matrix, start)


def body(grad_parts, master, moment, variance, plan, step):
    total = plan.shape[0]
    owned = master.shape[0]
    counting = jnp.arange(total, dtype=jnp.int32)
    matching = plan[None, :] == counting[:, None]
    matrix_of_slot = jnp.sum(jnp.where(matching, counting[None, :], 0), axis=1)
    ordered = jnp.take(grad_parts[0], matrix_of_slot, axis=0)
    slotted = lax.psum_scatter(ordered, ("side", "group"), scatter_dimension=0, tiled=True).astype(
        jnp.float32
    )
    new_moment = BETA_ONE * moment + (1.0 - BETA_ONE) * slotted
    new_variance = BETA_TWO * variance + (1.0 - BETA_TWO) * slotted * slotted
    my_slots = lax.axis_index(("side", "group")) * owned + jnp.arange(owned, dtype=jnp.int32)
    my_matrices = jnp.take(matrix_of_slot, my_slots, axis=0)
    count = jnp.take(step, my_matrices, axis=0).astype(jnp.float32)[:, None, None]
    first_fix = 1.0 - jnp.power(jnp.float32(BETA_ONE), count)
    second_fix = 1.0 - jnp.power(jnp.float32(BETA_TWO), count)
    update = new_moment / first_fix / (jnp.sqrt(new_variance / second_fix) + EPSILON)
    new_master = master - LEARN * (update + DECAY * master)
    rounded = new_master.astype(jnp.bfloat16)
    rows_all = spread(rounded, plan, total)
    flipped = jnp.swapaxes(rows_all, 1, 2)
    rollout_weights = lax.all_to_all(flipped, "shard", split_axis=1, concat_axis=2, tiled=True)
    return (new_master, new_moment, new_variance, rollout_weights)


def solution(mesh):
    return jax.shard_map(
        body,
        mesh=mesh,
        in_specs=(
            P(("side", "group"), None, "shard", None),
            P(("side", "group"), "shard", None),
            P(("side", "group"), "shard", None),
            P(("side", "group"), "shard", None),
            P(),
            P(),
        ),
        out_specs=(
            P(("side", "group"), "shard", None),
            P(("side", "group"), "shard", None),
            P(("side", "group"), "shard", None),
            P(None, "shard", None),
        ),
        check_vma=False,
    )
```

profile of v0, /device:TPU:1, one launch (start us, length us, event | category | flops | bytes accessed | tf_op | source)
XLA Modules:
  0.0 390.4 jit_solution(12581636103675443658)
XLA Ops:
  7.2 0.0 reduce-scatter.2.cloned.1.call-start
  7.2 0.8 select_reduce_fusion
  8.0 4.7 %gather_fusion = bf16[4,224,2048]{2,1,0:T(8,128)(2,1)} fusion(bf16[4,224,2048]{2,1,0:T(8,128)(2,1)} %bitcast.21, s32[1024]{0:T(1024)S(1)} %pad_clamp_fusion), kind=kCustom, calls=%fused_computation | custom fusion | bytes 7340048 | tf_op jit(solution)/shard_map/jit(_take)/gather | solution.py:38
  12.7 4.3 %broadcast_select_fusion.1 = bf16[4,224,2048]{2,1,0:T(8,128)(2,1)} fusion(bf16[4,224,2048]{2,1,0:T(8,128)(2,1)} %gather_fusion, pred[4]{0:T(512)(128)(4,1)S(1)} %compare_and_fusion), kind=kLoop, calls=%fused_computation.3 | loop fusion | flops 1835008 | bytes 7340036 | tf_op jit(solution)/shard_map/jit(_take)/select_n | solution.py:38
  17.0 0.0 copy-start.1
  17.0 0.0 copy-start
  17.0 0.0 reduce-scatter.2.cloned.1.call-update
  17.0 0.6 dynamic-slice.4
  18.3 0.0 copy-done.1
  18.3 0.6 dynamic-slice.5
  19.6 73.1 %reduce-scatter.2.cloned.1.call-done = bf16[1,224,2048]{2,1,0:T(8,128)(2,1)} async-done(((bf16[4,224,2048]{2,1,0:T(8,128)(2,1)}), bf16[1,224,2048]{2,1,0:T(8,128)(2,1)}) %reduce-scatter.2.cloned.1.call-update) | async-done | bytes 917520 | tf_op jit(solution)/shard_map/reduce_scatter | solution.py:39
  92.7 0.0 copy-done
  92.7 0.0 copy-start.2
  92.7 5.8 %fusion.3 = (bf16[1,224,2048]{2,1,0:T(8,128)(2,1)S(1)}, f32[1,224,2048]{2,1,0:T(8,128)}, f32[1,224,2048]{2,1,0:T(8,128)}, f32[1,224,2048]{2,1,0:T(8,128)}) fusion(f32[1,224,2048]{2,1,0:T(8,128)S(1)} %copy-done, f32[]{:T(128)} %bitcast.8, f32[]{:T(128)} %bitcast.7, bf16[1,224,2048]{2,1,0:T(8,128)(2,1)} %reduce-scatter.2.cloned.1.call-done, ...), kind=kLoop, calls=%fused_computation.16 | loop fusion | flops 7798784 | bytes 12845064 | tf_op jit(solution)/shard_map/convert_element_type | solution.py:51
  98.5 0.0 copy-done.2
  98.5 204.2 %while.17 = (s32[]{:T(128)}, bf16[4,224,2048]{2,1,0:T(8,128)(2,1)}, s32[4]{0:T(128)S(1)}, bf16[1,224,2048]{2,1,0:T(8,128)(2,1)S(1)}, s32[]{:T(128)}, /*index=5*/u32[]{:T(128)}, u32[]{:T(128)}, u32[]{:T(128)}, s32[]{:T(128)}) while((s32[]{:T(128)}, bf16[4,224,2048]{2,1,0:T(8,128)(2,1)}, s32[4]{0:T(128)S(1)}, ...), condition=%wide.region_4.5_spmd, body=%wide.region_2.4_spmd.sunk | while | flops 917515 | bytes 9175295 | solution.py:29
  98.5 0.0 all-reduce.2.cloned.1.call-start
  98.5 0.6 dynamic_slice.15
  99.7 1.0 broadcast_select_fusion.3
  100.7 0.0 all-reduce.2.cloned.1.call-update
  100.7 43.6 %all-reduce.2.cloned.1.call-done = bf16[1,224,2048]{2,1,0:T(8,128)(2,1)} async-done(((bf16[1,224,2048]{2,1,0:T(8,128)(2,1)}), bf16[1,224,2048]{2,1,0:T(8,128)(2,1)}) %all-reduce.2.cloned.1.call-update) | async-done | bytes 917520 | tf_op jit(solution)/shard_map/while/body/eval_jaxpr/psum | solution.py:15
  144.3 2.2 constant_dynamic-update-slice_fusion.2
  146.5 0.0 all-reduce.2.cloned.1.call-start
  146.5 0.6 dynamic_slice.15
  147.8 1.0 broadcast_select_fusion.3
  148.8 0.0 all-reduce.2.cloned.1.call-update
  148.8 47.8 %all-reduce.2.cloned.1.call-done = bf16[1,224,2048]{2,1,0:T(8,128)(2,1)} async-done(((bf16[1,224,2048]{2,1,0:T(8,128)(2,1)}), bf16[1,224,2048]{2,1,0:T(8,128)(2,1)}) %all-reduce.2.cloned.1.call-update) | async-done | bytes 917520 | tf_op jit(solution)/shard_map/while/body/eval_jaxpr/psum | solution.py:15
  196.6 2.2 constant_dynamic-update-slice_fusion.2
  198.8 0.0 all-reduce.2.cloned.1.call-start
  198.8 0.6 dynamic_slice.15
  200.0 1.0 broadcast_select_fusion.3
  201.0 0.0 all-reduce.2.cloned.1.call-update
  201.1 47.5 %all-reduce.2.cloned.1.call-done = bf16[1,224,2048]{2,1,0:T(8,128)(2,1)} async-done(((bf16[1,224,2048]{2,1,0:T(8,128)(2,1)}), bf16[1,224,2048]{2,1,0:T(8,128)(2,1)}) %all-reduce.2.cloned.1.call-update) | async-done | bytes 917520 | tf_op jit(solution)/shard_map/while/body/eval_jaxpr/psum | solution.py:15
  248.5 2.2 constant_dynamic-update-slice_fusion.2
  250.8 0.0 all-reduce.2.cloned.1.call-start
  250.8 0.6 dynamic_slice.15
  252.0 1.0 broadcast_select_fusion.3
  253.0 0.0 all-reduce.2.cloned.1.call-update
  253.0 47.5 %all-reduce.2.cloned.1.call-done = bf16[1,224,2048]{2,1,0:T(8,128)(2,1)} async-done(((bf16[1,224,2048]{2,1,0:T(8,128)(2,1)}), bf16[1,224,2048]{2,1,0:T(8,128)(2,1)}) %all-reduce.2.cloned.1.call-update) | async-done | bytes 917520 | tf_op jit(solution)/shard_map/while/body/eval_jaxpr/psum | solution.py:15
  300.5 2.2 constant_dynamic-update-slice_fusion.2
  302.7 7.3 %copy.17 = bf16[4,224,2048]{1,0,2:T(4,128)(2,1)} copy(bf16[4,224,2048]{2,1,0:T(8,128)(2,1)} %get-tuple-element.116) | data formatting | bytes 7340032 | tf_op jit(solution)/shard_map/while | solution.py:29
  310.0 60.1 %all_to_all.18 = bf16[4,2048,224]{2,0,1:T(4,128)(2,1)S(1)} all-to-all(bf16[4,2048,224]{2,0,1:T(4,128)(2,1)} %bitcast.20), channel_id=1, replica_groups=mesh['side'=2,'group'=2,'shard'=32] {'shard'}, dimensions={1} | all-to-all | bytes 7340032 | tf_op jit(solution)/shard_map/all_to_all | solution.py:54
  370.1 0.5 copy.18
  370.6 4.4 %copy.19 = bf16[4,64,32,224]{3,2,1,0:T(8,128)(2,1)} copy(bf16[4,64,32,224]{3,1,2,0:T(8,128)(2,1)S(1)} %bitcast.19) | data formatting | bytes 7340032 | tf_op jit(solution)/shard_map/all_to_all | solution.py:54
  375.0 8.8 %all_to_all.16 = bf16[4,64,7168]{2,1,0:T(8,128)(2,1)} reshape(bf16[4,64,32,224]{3,2,1,0:T(8,128)(2,1)} %copy.19) | data formatting | bytes 7340032 | tf_op jit(solution)/shard_map/all_to_all | solution.py:54
  (4 shorter events, 0.0 us)
Async XLA Ops:
  7.2 85.5 %reduce-scatter.2.cloned.1.call-start = ((), (), s32[]{:S(2)}) async-start(), calls=%async_computation.2 | async-start | bytes 4587520 | tf_op jit(solution)/shard_map/reduce_scatter | solution.py:39
  17.0 1.3 copy-start.1
  17.0 75.7 %copy-start = (f32[1,224,2048]{2,1,0:T(8,128)S(1)}, f32[1,224,2048]{2,1,0:T(8,128)}, u32[]{:S(2)}) copy-start(f32[1,224,2048]{2,1,0:T(8,128)} %param.9) | copy-start | bytes 5505028
  92.7 5.8 %copy-start.2 = (s32[4]{0:T(128)S(1)}, s32[4]{0:T(128)}, u32[]{:S(2)}) copy-start(s32[4]{0:T(128)} %param.12) | copy-start | bytes 52
  98.5 45.9 %all-reduce.2.cloned.1.call-start = ((), (), s32[]{:S(2)}) async-start(), calls=%async_computation.3 | async-start | bytes 1835008 | tf_op jit(solution)/shard_map/while/body/eval_jaxpr/psum | solution.py:15
  146.5 50.0 %all-reduce.2.cloned.1.call-start = ((), (), s32[]{:S(2)}) async-start(), calls=%async_computation.3 | async-start | bytes 1835008 | tf_op jit(solution)/shard_map/while/body/eval_jaxpr/psum | solution.py:15
  198.8 49.7 %all-reduce.2.cloned.1.call-start = ((), (), s32[]{:S(2)}) async-start(), calls=%async_computation.3 | async-start | bytes 1835008 | tf_op jit(solution)/shard_map/while/body/eval_jaxpr/psum | solution.py:15
  250.8 49.7 %all-reduce.2.cloned.1.call-start = ((), (), s32[]{:S(2)}) async-start(), calls=%async_computation.3 | async-start | bytes 1835008 | tf_op jit(solution)/shard_map/while/body/eval_jaxpr/psum | solution.py:15
Sparse Core Ops, SparseCore 0:
  17.1 75.5 reduce-scatter.1
  102.2 42.0 all-reduce.1
  150.3 46.2 all-reduce.1
  202.2 46.2 all-reduce.1
  254.2 46.2 all-reduce.1
where the time goes:
time: 391 us; the launch traced here: 390 us
  waiting for transfers between devices  260 us (66%)
  blocking collectives  60.1 us (15%)
  local copies, waits for them, and re-layouts  38 us (10%)
  between operations  15.2 us (4%)
  other arithmetic  14.8 us (4%)
    psum x4, waiting for transfers between devices, from_root(): return lax.psum(jnp.where(mine, shard, jnp.zeros_like(shard)), axis)  186 us
    reduce_scatter x1, waiting for transfers between devices, body(): lax.psum_scatter(ordered, ('side', 'group'), scatter_dimension=0, tiled=T...  73.1 us
    all_to_all x1, blocking collectives, body(): lax.all_to_all(flipped, 'shard', split_axis=1, concat_axis=2, tiled=True)  60.1 us
    all_to_all x3, local copies, waits for them, and re-layouts, body(): lax.all_to_all(flipped, 'shard', split_axis=1, concat_axis=2, tiled=True)  13.7 us
    dynamic_update_slice x4, local copies, waits for them, and re-layouts, one_matrix(): return lax.dynamic_update_index_in_dim(result, got, index, 0)  8.84 us
  transfers between devices with their start and end apart: 5, of which 5 were waited for; matrix products, arithmetic and copies ran while one was open for 0% of the time, Pallas kernels for 0%

commit v1 on v0

--- a/solution.py
+++ b/solution.py
@@ -12,7 +12,7 @@
 
 def from_root(shard, axis, root):
     mine = lax.axis_index(axis) == root
-    return lax.psum(jnp.where(mine, shard, jnp.zeros_like(shard)), axis)
+    return jnp.sum(lax.all_gather(jnp.where(mine, shard, jnp.zeros_like(shard)), axis), axis=0)
 
 
 def spread(local, plan, total):

time: 391 us -> 505 us (1.29)
  waiting for transfers between devices: 260 us -> 369 us
  other arithmetic: 14.8 us -> 26 us
    all_gather x0 -> x4, waiting for transfers between devices: none -> 295 us  [from_root(): lax.all_gather(jnp.where(mine, shard, jnp.zeros_like(shard)), axis)]
    psum x4 -> x0, waiting for transfers between devices: 186 us -> none  [from_root(): return lax.psum(jnp.where(mine, shard, jnp.zeros_like(shard)), axis)]
    reduce_sum x0 -> x4, other arithmetic: none -> 11.2 us  [from_root(): jnp.sum(lax.all_gather(jnp.where(mine, shard, jnp.zeros_like(shard)), axi...]
where the time goes in v1:
time: 505 us; the launch traced here: 504 us
  waiting for transfers between devices  369 us (73%)
  blocking collectives  58.3 us (12%)
  local copies, waits for them, and re-layouts  33.2 us (7%)
  other arithmetic  26 us (5%)
  between operations  15.2 us (3%)
    all_gather x4, waiting for transfers between devices, from_root(): lax.all_gather(jnp.where(mine, shard, jnp.zeros_like(shard)), axis)  295 us
    reduce_scatter x1, waiting for transfers between devices, body(): lax.psum_scatter(ordered, ('side', 'group'), scatter_dimension=0, tiled=T...  73.1 us
    all_to_all x1, blocking collectives, body(): lax.all_to_all(flipped, 'shard', split_axis=1, concat_axis=2, tiled=True)  58.3 us
    all_to_all x3, local copies, waits for them, and re-layouts, body(): lax.all_to_all(flipped, 'shard', split_axis=1, concat_axis=2, tiled=True)  13.7 us
    reduce_sum x4, other arithmetic, from_root(): jnp.sum(lax.all_gather(jnp.where(mine, shard, jnp.zeros_like(shard)), axi...  11.2 us
  transfers between devices with their start and end apart: 5, of which 5 were waited for; matrix products, arithmetic and copies ran while one was open for 0% of the time, Pallas kernels for 0%

profile of v1, /device:TPU:1, one launch (start us, length us, event | category | flops | bytes accessed | tf_op | source)
XLA Modules:
  0.0 504.0 jit_solution(2776942538774184148)
XLA Ops:
  7.2 0.0 reduce-scatter.2.cloned.1.call-start
  7.2 0.8 select_reduce_fusion
  8.0 4.7 gather_fusion
  12.7 4.3 broadcast_select_fusion.1
  17.0 0.0 copy-start.1
  17.0 0.0 copy-start
  17.0 0.0 reduce-scatter.2.cloned.1.call-update
  17.0 0.6 dynamic-slice.4
  18.3 0.0 copy-done.1
  18.3 0.6 dynamic-slice.5
  19.6 73.1 %reduce-scatter.2.cloned.1.call-done = bf16[1,224,2048]{2,1,0:T(8,128)(2,1)} async-done(((bf16[4,224,2048]{2,1,0:T(8,128)(2,1)}), bf16[1,224,2048]{2,1,0:T(8,128)(2,1)}) %reduce-scatter.2.cloned.1.call-update) | async-done | bytes 917520 | tf_op jit(solution)/shard_map/reduce_scatter | solution.py:39
  92.7 0.0 copy-done
  92.7 5.8 %fusion.3 = (bf16[1,224,2048]{2,1,0:T(8,128)(2,1)S(1)}, f32[1,224,2048]{2,1,0:T(8,128)}, f32[1,224,2048]{2,1,0:T(8,128)}, f32[1,224,2048]{2,1,0:T(8,128)}) fusion(f32[1,224,2048]{2,1,0:T(8,128)S(1)} %copy-done, f32[]{:T(128)} %bitcast.9, f32[]{:T(128)} %bitcast.8, bf16[1,224,2048]{2,1,0:T(8,128)(2,1)} %reduce-scatter.2.cloned.1.call-done, ...), kind=kLoop, calls=%fused_computation.16 | loop fusion | flops 7798784 | bytes 12845064 | tf_op jit(solution)/shard_map/convert_element_type | solution.py:51
  98.5 0.0 copy-done.2
  98.5 319.7 %while.17 = (s32[]{:T(128)}, bf16[4,224,2048]{2,1,0:T(8,128)(2,1)}, s32[4]{0:T(128)S(1)}, bf16[1,224,2048]{2,1,0:T(8,128)(2,1)S(1)}, s32[]{:T(128)}, /*index=5*/...) while((s32[]{:T(128)}, bf16[4,224,2048]{2,1,0:T(8,128)(2,1)}, s32[4]{0:T(128)S(1)}, ...), condition=%wide.region_4.5_spmd, body=%wide.region_2.4_spmd.sunk | while | flops 1835019 | bytes 22020360 | solution.py:29
  98.5 0.0 all-gather.2.cloned.1.call-start
  98.5 0.6 dynamic_slice.15
  99.7 1.0 broadcast_select_fusion.3
  100.7 0.0 all-gather.2.cloned.1.call-update
  100.7 72.8 %all-gather.2.cloned.1.call-done = bf16[4,224,2048]{2,1,0:T(8,128)(2,1)} async-done(((bf16[1,224,2048]{2,1,0:T(8,128)(2,1)}), bf16[4,224,2048]{2,1,0:T(8,128)(2,1)}) %all-gather.2.cloned.1.call-update) | async-done | bytes 3670032 | tf_op jit(solution)/shard_map/while/body/eval_jaxpr/all_gather | solution.py:15
  173.5 2.8 reduce_sum.29
  176.4 1.0 bitcast_dynamic-update-slice_fusion.2
  177.3 0.0 all-gather.2.cloned.1.call-start
  177.3 0.6 dynamic_slice.15
  178.6 1.0 broadcast_select_fusion.3
  179.6 0.0 all-gather.2.cloned.1.call-update
  179.6 74.4 %all-gather.2.cloned.1.call-done = bf16[4,224,2048]{2,1,0:T(8,128)(2,1)} async-done(((bf16[1,224,2048]{2,1,0:T(8,128)(2,1)}), bf16[4,224,2048]{2,1,0:T(8,128)(2,1)}) %all-gather.2.cloned.1.call-update) | async-done | bytes 3670032 | tf_op jit(solution)/shard_map/while/body/eval_jaxpr/all_gather | solution.py:15
  254.0 2.8 reduce_sum.29
  256.8 1.0 bitcast_dynamic-update-slice_fusion.2
  257.8 0.0 all-gather.2.cloned.1.call-start
  257.8 0.6 dynamic_slice.15
  259.1 1.0 broadcast_select_fusion.3
  260.0 0.0 all-gather.2.cloned.1.call-update
  260.1 74.1 %all-gather.2.cloned.1.call-done = bf16[4,224,2048]{2,1,0:T(8,128)(2,1)} async-done(((bf16[1,224,2048]{2,1,0:T(8,128)(2,1)}), bf16[4,224,2048]{2,1,0:T(8,128)(2,1)}) %all-gather.2.cloned.1.call-update) | async-done | bytes 3670032 | tf_op jit(solution)/shard_map/while/body/eval_jaxpr/all_gather | solution.py:15
  334.2 2.8 reduce_sum.29
  337.0 1.0 bitcast_dynamic-update-slice_fusion.2
  338.0 0.0 all-gather.2.cloned.1.call-start
  338.0 0.6 dynamic_slice.15
  339.2 1.0 broadcast_select_fusion.3
  340.2 0.0 all-gather.2.cloned.1.call-update
  340.2 74.1 %all-gather.2.cloned.1.call-done = bf16[4,224,2048]{2,1,0:T(8,128)(2,1)} async-done(((bf16[1,224,2048]{2,1,0:T(8,128)(2,1)}), bf16[4,224,2048]{2,1,0:T(8,128)(2,1)}) %all-gather.2.cloned.1.call-update) | async-done | bytes 3670032 | tf_op jit(solution)/shard_map/while/body/eval_jaxpr/all_gather | solution.py:15
  414.3 2.8 reduce_sum.29
  417.1 1.0 bitcast_dynamic-update-slice_fusion.2
  418.1 7.3 %copy.17 = bf16[4,224,2048]{1,0,2:T(4,128)(2,1)} copy(bf16[4,224,2048]{2,1,0:T(8,128)(2,1)} %get-tuple-element.117) | data formatting | bytes 7340032 | tf_op jit(solution)/shard_map/while | solution.py:29
  425.4 58.3 %all_to_all.18 = bf16[4,2048,224]{2,0,1:T(4,128)(2,1)S(1)} all-to-all(bf16[4,2048,224]{2,0,1:T(4,128)(2,1)} %bitcast.24), channel_id=1, replica_groups=mesh['side'=2,'group'=2,'shard'=32] {'shard'}, dimensions={1} | all-to-all | bytes 7340032 | tf_op jit(solution)/shard_map/all_to_all | solution.py:54
  483.7 0.5 copy.18
  484.3 4.4 copy.19
  488.7 8.8 %all_to_all.16 = bf16[4,64,7168]{2,1,0:T(8,128)(2,1)} reshape(bf16[4,64,32,224]{3,2,1,0:T(8,128)(2,1)} %copy.19) | data formatting | bytes 7340032 | tf_op jit(solution)/shard_map/all_to_all | solution.py:54
  (5 shorter events, 0.0 us)
Async XLA Ops:
  7.2 85.5 %reduce-scatter.2.cloned.1.call-start = ((), (), s32[]{:S(2)}) async-start(), calls=%async_computation.2 | async-start | bytes 4587520 | tf_op jit(solution)/shard_map/reduce_scatter | solution.py:39
  17.0 1.3 copy-start.1
  17.0 75.7 %copy-start = (f32[1,224,2048]{2,1,0:T(8,128)S(1)}, f32[1,224,2048]{2,1,0:T(8,128)}, u32[]{:S(2)}) copy-start(f32[1,224,2048]{2,1,0:T(8,128)} %param.9) | copy-start | bytes 5505028
  92.7 5.8 %copy-start.2 = (s32[4]{0:T(128)S(1)}, s32[4]{0:T(128)}, u32[]{:S(2)}) copy-start(s32[4]{0:T(128)} %param.12) | copy-start | bytes 52
  98.5 75.1 %all-gather.2.cloned.1.call-start = ((), (), s32[]{:S(2)}) async-start(), calls=%async_computation.3 | async-start | bytes 4587520 | tf_op jit(solution)/shard_map/while/body/eval_jaxpr/all_gather | solution.py:15
  177.3 76.6 %all-gather.2.cloned.1.call-start = ((), (), s32[]{:S(2)}) async-start(), calls=%async_computation.3 | async-start | bytes 4587520 | tf_op jit(solution)/shard_map/while/body/eval_jaxpr/all_gather | solution.py:15
  257.8 76.3 %all-gather.2.cloned.1.call-start = ((), (), s32[]{:S(2)}) async-start(), calls=%async_computation.3 | async-start | bytes 4587520 | tf_op jit(solution)/shard_map/while/body/eval_jaxpr/all_gather | solution.py:15
  338.0 76.3 %all-gather.2.cloned.1.call-start = ((), (), s32[]{:S(2)}) async-start(), calls=%async_computation.3 | async-start | bytes 4587520 | tf_op jit(solution)/shard_map/while/body/eval_jaxpr/all_gather | solution.py:15
Sparse Core Ops, SparseCore 0:
  17.1 75.5 reduce-scatter.1
  101.5 71.9 all-gather.1
  180.4 73.5 all-gather.1
  260.5 73.5 all-gather.1
  340.7 73.5 all-gather.1
